TPU v7x, 32 devices: a whole 2x2x4 slice. The times are simulated.
32 devices in a mesh: front: 4 (over y, x), row: 4 (over z), col: 2 (over core).
Axes of the slice: x: 2, y: 2, z: 4, core: 2. Of those that a mesh axis runs over, the one named last changes fastest.
Arguments:
- front_in: float32 [32768, 8192], P(('front', 'row'), 'col'), parts along dimension 0, may hold values from -6 to 6
- child_tiles: bfloat16 [32, 56, 128, 128], P(('front', 'row', 'col')), parts along dimension 0, may hold values from -6 to 6
- child_map: int32 [32, 56], P(('front', 'row', 'col')), parts along dimension 0, may hold values from 0 to 4095, as said below
- pattern: int32 [256, 64], P('front'), parts along dimension 0, may hold values 0 or 1
- pivot_inverse: float32 [8, 512, 512], P('front'), parts along dimension 0, may hold values from -0.01171875 to 0.01171875
Outputs:
- front_out: float32 [32768, 8192], P(('front', 'row'), 'col'), parts along dimension 0
There are 4 independent parts, one for each index of `front`. A program takes and returns all parts, laid end to end along the dimension named above; each array names one. Nothing has to cross between parts.
Inputs may be any that keep to these rules, and one draw needn't show every extreme that they name: Entries j * 7 to (j + 1) * 7 - 1 of each row of child_map name tiles held by device j of the front's grid, j = grid row * 2 + grid column, that device holding tile rows of its 2048 rows and tile columns of its 4096 columns.
All inputs are finite; a program needn't handle non-finite values.
Results may differ from a plain program's by a relative error of at most 0.0062.
Values may be sent and summed in bfloat16 or wider, within the bound.
No kernel may reach another device: no remote copies, remote signals or barrier semaphores. Data moves between devices by JAX's collectives and lax.ppermute only.
A program may use at most 256 MiB of HBM per device.

v0:
```python
import jax
import jax.numpy as jnp
from jax import lax
from jax.sharding import PartitionSpec as P

TILE = 128
PANEL = 512
PANELS = 2
SLOTS = 7
NT = 64


def spread(x, axis, root):
    mine = lax.axis_index(axis) == root
    return lax.psum(jnp.where(mine, x, jnp.zeros_like(x)), axis)


def factor_panel(matrix, inverse, panel_index):
    first_col = panel_index * PANEL
    lower_part = jnp.dot(
        matrix[:, first_col : first_col + PANEL],
        inverse[panel_index],
        precision=lax.Precision.HIGHEST,
        preferred_element_type=jnp.float32,
    )
    shared = spread(lower_part.astype(jnp.bfloat16), "col", 0)
    return (lower_part, shared)


def apply_update(
    matrix, shared, upper_rows, finish, first_col, last_col, row_global, col_global, tile_mask
):
    row_count = matrix.shape[0]
    product = jnp.dot(shared, upper_rows, preferred_element_type=jnp.float32)
    width = last_col - first_col
    product = (
        product.reshape(row_count // TILE, TILE, width // TILE, TILE) * tile_mask[:, None, :, None]
    ).reshape(row_count, width)
    active_mask = (row_global >= finish)[:, None] & (col_global >= finish)[None, :]
    return matrix.at[:, first_col:last_col].add(-jnp.where(active_mask, product, 0.0))


def body(front_in, child_tiles, child_map, pattern, pivot_inverse):
    row_count, col_count = front_in.shape
    grid_rows = lax.axis_size("row")
    grid_cols = lax.axis_size("col")
    groups = grid_rows * grid_cols
    row_index = lax.axis_index("row")
    col_index = lax.axis_index("col")
    tile_rows = row_count // TILE
    tile_cols = col_count // TILE
    outgoing = child_tiles.reshape(grid_rows, grid_cols, SLOTS, TILE, TILE)
    targets = child_map.reshape(grid_rows, grid_cols, SLOTS)
    arrived, placed = (
        lax.all_to_all(
            outgoing.reshape(groups, SLOTS, TILE, TILE),
            ("row", "col"),
            split_axis=0,
            concat_axis=0,
            tiled=True,
        ),
        lax.all_to_all(
            targets.reshape(groups, SLOTS), ("row", "col"), split_axis=0, concat_axis=0, tiled=True
        ),
    )
    child_flat = arrived.reshape(-1, TILE, TILE).astype(jnp.float32)
    flat_targets = placed.reshape(-1)
    local_row = flat_targets // NT - row_index * tile_rows
    local_col = flat_targets % NT - col_index * tile_cols
    matrix = (
        front_in.reshape(tile_rows, TILE, tile_cols, TILE)
        .at[local_row, :, local_col, :]
        .add(child_flat)
        .reshape(row_count, col_count)
    )
    row_global = row_index * row_count + jnp.arange(row_count)
    col_global = col_index * col_count + jnp.arange(col_count)
    tile_mask = lax.dynamic_slice(
        pattern, (row_index * tile_rows, col_index * tile_cols), (tile_rows, tile_cols)
    ).astype(jnp.float32)
    lower_part, shared = factor_panel(matrix, pivot_inverse, 0)
    for panel_index in range(PANELS):
        first_col = panel_index * PANEL
        finish = first_col + PANEL
        upper_rows = spread(matrix[first_col:finish, :].astype(jnp.bfloat16), "row", 0)
        stored = (row_global >= finish)[:, None] & (col_index == 0)
        matrix = matrix.at[:, first_col:finish].set(
            jnp.where(stored, lower_part, matrix[:, first_col:finish])
        )
        matrix = apply_update(
            matrix, shared, upper_rows, finish, 0, col_count, row_global, col_global, tile_mask
        )
        following = (
            factor_panel(matrix, pivot_inverse, panel_index + 1)
            if panel_index + 1 < PANELS
            else (lower_part, shared)
        )
        lower_part, shared = following
    return matrix


def solution(mesh):
    placed = (
        P(("front", "row"), "col"),
        P(("front", "row", "col"), None, None, None),
        P(("front", "row", "col"), None),
        P("front", None),
        P("front", None, None),
    )
    return jax.shard_map(
        body, mesh=mesh, in_specs=placed, out_specs=P(("front", "row"), "col"), check_vma=False
    )
```

profile of v0, /device:TPU:0, one launch (start us, length us, event | category | flops | bytes accessed | tf_op | source)
XLA Modules:
  0.0 648.1 jit_solution(2645045330365781830)
XLA Ops:
  6.5 0.6 broadcast.330
  7.1 1.4 reduce.28
  8.6 11.7 %all_to_all.14 = s32[8,1,7]{2,1,0:T(1,128)S(1)} all-to-all(s32[8,1,7]{2,1,0:T(1,128)S(1)} %bitcast.61), channel_id=1, replica_groups=mesh['front'=4,'row'=4,'col'=2] {'row','col'}, dimensions={0} | all-to-all | bytes 448 | tf_op jit(solution)/shard_map/all_to_all | solution.py:62
  20.3 3.6 all-to-all-start.1
  24.0 17.2 %copy.14 = f32[256,8,32,128]{3,2,1,0:T(8,128)S(1)} copy(f32[256,8,32,128]{3,1,2,0:T(8,128)} %bitcast.57) | data formatting | bytes 67108864
  41.2 21.6 %copy.11 = f32[16,128,32,128]{3,1,2,0:T(8,128)} copy(f32[16,128,32,128]{3,2,1,0:T(8,128)S(1)} %bitcast.55) | data formatting | bytes 67108864 | tf_op jit(solution)/shard_map/reshape | solution.py:71
  62.8 0.7 reduce.29
  63.6 3.7 all-to-all-done.1
  67.2 2.4 bitcast_convert_fusion
  69.6 13.5 %scatter_fusion = f32[16,128,32,128]{3,1,2,0:T(8,128)} fusion(f32[16,128,32,128]{3,1,2,0:T(8,128)} %copy.11, s32[56]{0:T(128)S(1)} %fusion.24, f32[56,128,128]{2,1,0:T(8,128)} %bitcast_convert_fusion), kind=kCustom, calls=%fused_computation | custom fusion | flops 917504 | bytes 11010496 | tf_op jit(solution)/shard_map/scatter-add | solution.py:73
  83.1 31.7 %copy.12 = f32[16,128,32,128]{3,2,1,0:T(8,128)} copy(f32[16,128,32,128]{3,1,2,0:T(8,128)} %scatter_fusion) | data formatting | bytes 67108864 | tf_op jit(solution)/shard_map/scatter-add | solution.py:73
  114.8 36.4 %copy.22 = f32[256,8,32,128]{3,1,2,0:T(8,128)S(1)} copy(f32[256,8,32,128]{3,2,1,0:T(8,128)} %bitcast.56) | data formatting | bytes 67108864
  151.3 11.1 %copy-done = f32[256,8,32,128]{3,1,2,0:T(8,128)} copy-done((f32[256,8,32,128]{3,1,2,0:T(8,128)}, f32[256,8,32,128]{3,1,2,0:T(8,128)S(1)}, u32[]{:S(2)}) %copy-start) | copy-done | bytes 33554456
  162.3 8.6 %convert_select_fusion.1 = (bf16[2048,512]{1,0:T(8,128)(2,1)}, f32[2048,512]{1,0:T(8,128)}) fusion(pred[]{:T(512)S(6)} %eq.6, f32[2,512,512]{2,1,0:T(8,128)S(1)} %copy-done.2, f32[2048,4096]{1,0:T(8,128)S(1)} %bitcast.53), kind=kOutput, calls=%fused_computation.24 | convolution fusion | flops 6444548096 | bytes 11534337 | tf_op jit(solution)/shard_map/dot_general | solution.py:20
  171.2 3.8 fusion.8
  175.0 2.7 copy.13
  177.7 6.2 copy.23
  183.9 0.3 all-reduce.9.cloned.1.call-start
  184.2 0.6 compare_reduce_fusion.1
  184.9 0.8 dynamic-slice_convert_fusion
  185.6 7.3 %fusion.6 = f32[2048,4096]{1,0:T(8,128)} fusion(f32[2048,4096]{1,0:T(8,128)} %bitcast.54, f32[2048,512]{1,0:T(8,128)} %get-tuple-element.70, pred[2048]{0:T(1024)(128)(4,1)S(1)} %get-tuple-element.76, pred[]{:T(512)} %compare_reduce_fusion.1), kind=kLoop, calls=%fused_computation.14 | loop fusion | flops 2097152 | bytes 12585472 | tf_op jit(solution)/shard_map/scatter | solution.py:87
  192.9 157.0 %all-reduce.7.cloned.1.call-done = bf16[512,4096]{1,0:T(8,128)(2,1)} async-done(((bf16[512,4096]{1,0:T(8,128)(2,1)}), bf16[512,4096]{1,0:T(8,128)(2,1)}) %all-reduce.7.cloned.1.call-update) | async-done | bytes 4194320 | tf_op jit(solution)/shard_map/psum | solution.py:15
  349.9 11.3 %mul.36 = f32[16,128,32,128]{3,2,1,0:T(8,128)} broadcast(f32[16,32]{1,0:T(8,128)S(1)} %dynamic-slice_convert_fusion), dimensions={0,2} | broadcast | bytes 33556480 | tf_op jit(solution)/shard_map/mul | solution.py:37
  361.2 42.8 %fusion.2 = f32[2048,4096]{1,0:T(8,128)} fusion(f32[2048,4096]{1,0:T(8,128)} %fusion.6, f32[256,8,32,128]{3,2,1,0:T(8,128)} %bitcast.51, bf16[2048,512]{1,0:T(8,128)(2,1)S(1)} %copy-done.1, bf16[512,4096]{1,0:T(8,128)(2,1)} %all-reduce.7.cloned.1.call-done, pred[4096]{0:T(1024)(128)(4,1)S(1)} %fusion.19, pred[2048]{0:T(1024)(128)(4,1)S(1)} %get-tuple-element.75), kind=kOutput, calls=%fused_computation.5 | convolution fusion | flops 8631877632 | bytes 106960896 | tf_op jit(solution)/shard_map/dot_general | solution.py:34
  404.0 10.4 %convert_select_fusion = (bf16[2048,512]{1,0:T(8,128)(2,1)}, f32[2048,512]{1,0:T(8,128)}) fusion(pred[]{:T(512)S(6)} %eq.6, f32[2,512,512]{2,1,0:T(8,128)} %param.21, f32[2048,4096]{1,0:T(8,128)} %fusion.2), kind=kOutput, calls=%fused_computation.23 | convolution fusion | flops 6444548096 | bytes 11534337 | tf_op jit(solution)/shard_map/dot_general | solution.py:20
  414.5 0.5 all-reduce.11.cloned.1.call-start
  415.0 5.7 fusion.9
  420.7 0.7 compare_reduce_fusion
  421.4 5.8 fusion.7
  427.2 7.6 %all-reduce.9.cloned.1.call-done = bf16[2048,512]{1,0:T(8,128)(2,1)} async-done(((bf16[2048,512]{1,0:T(8,128)(2,1)}), bf16[2048,512]{1,0:T(8,128)(2,1)}) %all-reduce.9.cloned.1.call-update) | async-done | bytes 2097168 | tf_op jit(solution)/shard_map/psum | solution.py:15
  434.9 158.4 %all-reduce.11.cloned.1.call-done = bf16[512,4096]{1,0:T(8,128)(2,1)} async-done(((bf16[512,4096]{1,0:T(8,128)(2,1)}), bf16[512,4096]{1,0:T(8,128)(2,1)}) %all-reduce.11.cloned.1.call-update) | async-done | bytes 4194320 | tf_op jit(solution)/shard_map/psum | solution.py:15
  593.3 48.2 %fusion.5 = f32[2048,4096]{1,0:T(8,128)} fusion(f32[2048,4096]{1,0:T(8,128)} %fusion.7, f32[256,8,32,128]{3,2,1,0:T(8,128)} %bitcast.52, bf16[2048,512]{1,0:T(8,128)(2,1)} %all-reduce.9.cloned.1.call-done, bf16[512,4096]{1,0:T(8,128)(2,1)} %all-reduce.11.cloned.1.call-done, pred[4096]{0:T(1024)(128)(4,1)S(1)} %fusion.18, ...), kind=kOutput, calls=%fused_computation.8 | convolution fusion | flops 8631877632 | bytes 106960896 | tf_op jit(solution)/shard_map/dot_general | solution.py:34
  (19 shorter events, 0.6 us)
Async XLA Ops:
  20.3 46.9 %all-to-all-start.1 = ((bf16[8,7,128,128]{3,2,1,0:T(8,128)(2,1)}), bf16[8,7,128,128]{3,2,1,0:T(8,128)(2,1)S(1)}, u32[]{:S(2)}, u32[]{:S(2)}) async-start(bf16[8,7,128,128]{3,2,1,0:T(8,128)(2,1)} %bitcast.60), calls=%async_computation.1 | async-start | bytes 3670016 | tf_op jit(solution)/shard_map/all_to_all | solution.py:55
  23.9 169.0 %all-reduce.5.cloned.1.call-start = ((), (), s32[]{:S(2)}) async-start(), calls=%async_computation.2 | async-start | bytes 4194304 | tf_op jit(solution)/shard_map/psum | solution.py:15
  114.8 47.5 %copy-start.2 = (f32[2,512,512]{2,1,0:T(8,128)S(1)}, f32[2,512,512]{2,1,0:T(8,128)}, u32[]{:S(2)}) copy-start(f32[2,512,512]{2,1,0:T(8,128)} %param.21) | copy-start | bytes 6291460
  151.3 11.1 %copy-start = (f32[256,8,32,128]{3,1,2,0:T(8,128)}, f32[256,8,32,128]{3,1,2,0:T(8,128)S(1)}, u32[]{:S(2)}) copy-start(f32[256,8,32,128]{3,1,2,0:T(8,128)S(1)} %copy.22) | copy-start | bytes 100663296
  170.9 179.0 %all-reduce.7.cloned.1.call-start = ((), (), s32[]{:S(2)}) async-start(), calls=%async_computation.3 | async-start | bytes 8388608 | tf_op jit(solution)/shard_map/psum | solution.py:15
  183.9 251.0 %all-reduce.9.cloned.1.call-start = ((), (), s32[]{:S(2)}) async-start(), calls=%async_computation.4 | async-start | bytes 4194304 | tf_op jit(solution)/shard_map/psum | solution.py:15
  192.9 168.3 %copy-start.1 = (bf16[2048,512]{1,0:T(8,128)(2,1)S(1)}, bf16[2048,512]{1,0:T(8,128)(2,1)}, u32[]{:S(2)}) copy-start(bf16[2048,512]{1,0:T(8,128)(2,1)} %all-reduce.5.cloned.1.call-done) | copy-start | bytes 6291460
  414.5 178.8 %all-reduce.11.cloned.1.call-start = ((), (), s32[]{:S(2)}) async-start(), calls=%async_computation.5 | async-start | bytes 8388608 | tf_op jit(solution)/shard_map/psum | solution.py:15
Sparse Core Ops, SparseCore 0:
  171.0 20.2 all-reduce.4
  193.7 156.1 all-reduce.6
  414.6 20.2 all-reduce.8
  437.1 156.1 all-reduce.10
where the time goes:
time: 656 us; the launch traced here: 648 us
  waiting for transfers between devices  327 us (50%)
  local copies, waits for them, and re-layouts  139 us (21%)
  matrix products  110 us (17%)
  other arithmetic  42.7 us (7%)
  between operations  13.4 us (2%)
  blocking collectives  11.7 us (2%)
    psum x4, waiting for transfers between devices, spread(): return lax.psum(jnp.where(mine, x, jnp.zeros_like(x)), axis)  323 us
    dot_general x2, matrix products, apply_update(): product = jnp.dot(shared, upper_rows, preferred_element_type=jnp.float32)  91 us
    unnamed x10, local copies, waits for them, and re-layouts  71.5 us
    scatter-add x1, local copies, waits for them, and re-layouts, body(): matrix = front_in.reshape(tile_rows, TILE, tile_cols, TILE).at[local_row,...  31.7 us
    reshape x1, local copies, waits for them, and re-layouts, body(): front_in.reshape(tile_rows, TILE, tile_cols, TILE)  21.6 us
    dot_general x2, matrix products, factor_panel(): jnp.dot(matrix[:, first_col:first_col + PANEL], inverse[panel_index], pre...  19 us
    scatter-add x1, other arithmetic, body(): matrix = front_in.reshape(tile_rows, TILE, tile_cols, TILE).at[local_row,...  13.5 us
  transfers between devices with their start and end apart: 5, of which 4 were waited for; matrix products, arithmetic and copies ran while one was open for 11% of the time, Pallas kernels for 0%

commit v1 on v0

--- a/solution.py
+++ b/solution.py
@@ -12,7 +12,7 @@
 
 def spread(x, axis, root):
     mine = lax.axis_index(axis) == root
-    return lax.psum(jnp.where(mine, x, jnp.zeros_like(x)), axis)
+    return jnp.sum(lax.all_gather(jnp.where(mine, x, jnp.zeros_like(x)), axis), axis=0)
 
 
 def factor_panel(matrix, inverse, panel_index):

time: 656 us -> 1020 us (1.55)
  waiting for transfers between devices: 327 us -> 561 us
  other arithmetic: 42.7 us -> 163 us
  local copies, waits for them, and re-layouts: 139 us -> 207 us
  matrix products: 110 us -> 50.2 us
    all_gather x0 -> x4, waiting for transfers between devices: none -> 557 us  [spread(): lax.all_gather(jnp.where(mine, x, jnp.zeros_like(x)), axis)]
    psum x4 -> x0, waiting for transfers between devices: 323 us -> none  [spread(): return lax.psum(jnp.where(mine, x, jnp.zeros_like(x)), axis)]
    add x0 -> x2, other arithmetic: none -> 87 us  [apply_update(): matrix.at[:, first_col:last_col].add(-jnp.where(active_mask, product, 0.0))]
    dot_general x2, matrix products: 91 us -> 31.5 us  [apply_update(): product = jnp.dot(shared, upper_rows, preferred_element_type=jnp.float32)]
    mul x1 -> x2, local copies, waits for them, and re-layouts: 11.3 us -> 63.4 us  [apply_update(): product.reshape(row_count // TILE, TILE, width // TILE, TILE)]
    reduce_sum x0 -> x4, other arithmetic: none -> 33.7 us  [spread(): jnp.sum(lax.all_gather(jnp.where(mine, x, jnp.zeros_like(x)), axis), axis=0)]
    dot_general x0 -> x2, local copies, waits for them, and re-layouts: none -> 12.9 us  [apply_update(): product = jnp.dot(shared, upper_rows, preferred_element_type=jnp.float32)]
    unnamed x10 -> x7, local copies, waits for them, and re-layouts: 71.5 us -> 65.3 us
  transfers between devices with their start and end apart: 5 -> 5, of which waited for: 4 -> 3; matrix products, arithmetic and copies ran while one was open for 11% -> 9% of each run, Pallas kernels for 0% -> 0%
where the time goes in v1:
time: 1020 us; the launch traced here: 1010 us
  waiting for transfers between devices  561 us (55%)
  local copies, waits for them, and re-layouts  207 us (20%)
  other arithmetic  163 us (16%)
  matrix products  50.2 us (5%)
  between operations  13.5 us (1%)
  blocking collectives  11.7 us (1%)
    all_gather x4, waiting for transfers between devices, spread(): lax.all_gather(jnp.where(mine, x, jnp.zeros_like(x)), axis)  557 us
    add x2, other arithmetic, apply_update(): matrix.at[:, first_col:last_col].add(-jnp.where(active_mask, product, 0.0))  87 us
    unnamed x7, local copies, waits for them, and re-layouts  65.3 us
    mul x2, local copies, waits for them, and re-layouts, apply_update(): product.reshape(row_count // TILE, TILE, width // TILE, TILE)  63.4 us
    reduce_sum x4, other arithmetic, spread(): jnp.sum(lax.all_gather(jnp.where(mine, x, jnp.zeros_like(x)), axis), axis=0)  33.7 us
    scatter-add x1, local copies, waits for them, and re-layouts, body(): matrix = front_in.reshape(tile_rows, TILE, tile_cols, TILE).at[local_row,...  31.7 us
    dot_general x2, matrix products, apply_update(): product = jnp.dot(shared, upper_rows, preferred_element_type=jnp.float32)  31.5 us
    reshape x1, local copies, waits for them, and re-layouts, body(): front_in.reshape(tile_rows, TILE, tile_cols, TILE)  21.6 us
  transfers between devices with their start and end apart: 5, of which 3 were waited for; matrix products, arithmetic and copies ran while one was open for 9% of the time, Pallas kernels for 0%

profile of v1, /device:TPU:0, one launch (start us, length us, event | category | flops | bytes accessed | tf_op | source)
XLA Modules:
  0.0 1010.0 jit_solution(2631259154058744783)
XLA Ops:
  8.6 11.7 %all_to_all.14 = s32[8,1,7]{2,1,0:T(1,128)S(1)} all-to-all(s32[8,1,7]{2,1,0:T(1,128)S(1)} %bitcast.85), channel_id=1, replica_groups=mesh['front'=4,'row'=4,'col'=2] {'row','col'}, dimensions={0} | all-to-all | bytes 448 | tf_op jit(solution)/shard_map/all_to_all | solution.py:62
  20.3 3.6 all-to-all-start.1
  24.0 17.2 %copy.26 = f32[256,8,32,128]{3,2,1,0:T(8,128)S(1)} copy(f32[256,8,32,128]{3,1,2,0:T(8,128)} %bitcast.74) | data formatting | bytes 67108864
  41.2 21.6 %copy.15 = f32[16,128,32,128]{3,1,2,0:T(8,128)} copy(f32[16,128,32,128]{3,2,1,0:T(8,128)S(1)} %bitcast.70) | data formatting | bytes 67108864 | tf_op jit(solution)/shard_map/reshape | solution.py:71
  63.6 3.7 all-to-all-done.1
  67.2 2.4 bitcast_convert_fusion
  69.6 13.5 %scatter_fusion = f32[16,128,32,128]{3,1,2,0:T(8,128)} fusion(f32[16,128,32,128]{3,1,2,0:T(8,128)} %copy.15, s32[56]{0:T(128)S(1)} %fusion.22, f32[56,128,128]{2,1,0:T(8,128)} %bitcast_convert_fusion), kind=kCustom, calls=%fused_computation | custom fusion | flops 917504 | bytes 11010496 | tf_op jit(solution)/shard_map/scatter-add | solution.py:73
  83.1 31.7 %copy.16 = f32[16,128,32,128]{3,2,1,0:T(8,128)} copy(f32[16,128,32,128]{3,1,2,0:T(8,128)} %scatter_fusion) | data formatting | bytes 67108864 | tf_op jit(solution)/shard_map/scatter-add | solution.py:73
  114.8 36.4 %copy.33 = f32[256,8,32,128]{3,1,2,0:T(8,128)S(1)} copy(f32[256,8,32,128]{3,2,1,0:T(8,128)} %bitcast.71) | data formatting | bytes 67108864
  151.3 11.1 %copy-done = f32[256,8,32,128]{3,1,2,0:T(8,128)} copy-done((f32[256,8,32,128]{3,1,2,0:T(8,128)}, f32[256,8,32,128]{3,1,2,0:T(8,128)S(1)}, u32[]{:S(2)}) %copy-start) | copy-done | bytes 33554456
  162.3 8.6 convert_select_fusion.1
  171.0 3.8 fusion.6
  174.8 4.8 copy.17
  179.6 7.3 select_n.119
  188.7 5.8 fusion.4
  194.5 5.7 reduce_sum.48
  200.1 273.1 %all-gather.8.cloned.1.call-done = bf16[4,512,4096]{2,1,0:T(8,128)(2,1)} async-done(((bf16[1,512,4096]{2,1,0:T(8,128)(2,1)}), bf16[4,512,4096]{2,1,0:T(8,128)(2,1)}) %all-gather.8.cloned.1.call-update) | async-done | bytes 16777232 | tf_op jit(solution)/shard_map/all_gather | solution.py:15
  473.3 11.9 %reduce_sum.49 = bf16[512,4096]{1,0:T(8,128)(2,1)} reduce(bf16[4,512,4096]{2,1,0:T(8,128)(2,1)} %all-gather.8.cloned.1.call-done, bf16[]{:T(256)} %constant.184.clone.1), dimensions={0}, to_apply=%region_3.4 | reduce | flops 6291456 | bytes 20971522 | tf_op jit(solution)/shard_map/reduce_sum | solution.py:15
  485.1 6.4 copy.24
  491.6 16.2 %broadcast_multiply_fusion.1 = f32[16,128,32,128]{3,1,2,0:T(8,128)} fusion(f32[16,32]{1,0:T(8,128)S(1)} %dynamic-slice_convert_fusion, bf16[16,128,512,1]{2,1,3,0:T(8,128)(2,1)} %bitcast.83, bf16[32,128,512,1]{2,1,0,3:T(8,128)(2,1)} %bitcast.81), kind=kOutput, calls=%fused_computation.9 | convolution fusion | flops 8598323200 | bytes 39847936 | tf_op jit(solution)/shard_map/dot_general | solution.py:34
  507.8 31.7 %copy.19 = f32[16,128,32,128]{3,2,1,0:T(8,128)} copy(f32[16,128,32,128]{3,1,2,0:T(8,128)} %broadcast_multiply_fusion.1) | data formatting | bytes 67108864 | tf_op jit(solution)/shard_map/mul | solution.py:37
  539.5 43.6 %fusion.3 = f32[2048,4096]{1,0:T(8,128)} fusion(f32[2048,4096]{1,0:T(8,128)} %fusion.4, f32[256,8,32,128]{3,2,1,0:T(8,128)} %bitcast.72, pred[4096]{0:T(1024)(128)(4,1)S(1)} %fusion.17, pred[2048]{0:T(1024)(128)(4,1)S(1)} %fusion.19), kind=kLoop, calls=%fused_computation.6 | loop fusion | flops 33554432 | bytes 100669440 | tf_op jit(solution)/shard_map/add | solution.py:40
  583.1 10.1 %convert_select_fusion = (bf16[2048,512]{1,0:T(8,128)(2,1)}, f32[2048,512]{1,0:T(8,128)}) fusion(pred[]{:T(512)S(6)} %eq.6, f32[2,512,512]{2,1,0:T(8,128)S(1)} %copy-done.1, f32[2048,4096]{1,0:T(8,128)} %fusion.3), kind=kOutput, calls=%fused_computation.22 | convolution fusion | flops 6444548096 | bytes 11534337 | tf_op jit(solution)/shard_map/dot_general | solution.py:20
  593.3 5.8 fusion.7
  600.0 6.5 fusion.5
  606.5 4.4 reduce_sum.50
  610.9 283.7 %all-gather.14.cloned.1.call-done = bf16[2048,4096]{1,0:T(8,128)(2,1)} async-done(((bf16[512,4096]{1,0:T(8,128)(2,1)}), bf16[2048,4096]{1,0:T(8,128)(2,1)}) %all-gather.14.cloned.1.call-update) | async-done | bytes 16777232 | tf_op jit(solution)/shard_map/all_gather | solution.py:15
  894.6 11.8 %reduce_sum.51 = bf16[512,4096]{1,0:T(8,128)(2,1)} reduce(bf16[4,512,4096]{2,1,0:T(8,128)(2,1)} %bitcast.75, bf16[]{:T(256)} %constant.184.clone.1), dimensions={0}, to_apply=%region_6.7 | reduce | flops 6291456 | bytes 20971522 | tf_op jit(solution)/shard_map/reduce_sum | solution.py:15
  906.4 6.4 copy.25
  912.8 15.2 %broadcast_multiply_fusion = f32[16,128,32,128]{3,1,2,0:T(8,128)} fusion(f32[16,32]{1,0:T(8,128)S(1)} %dynamic-slice_convert_fusion, bf16[16,128,512,1]{2,1,3,0:T(8,128)(2,1)S(1)} %bitcast.82, bf16[32,128,512,1]{2,1,0,3:T(8,128)(2,1)} %bitcast.80), kind=kOutput, calls=%fused_computation.8 | convolution fusion | flops 8598323200 | bytes 39847936 | tf_op jit(solution)/shard_map/dot_general | solution.py:34
  928.1 31.7 %copy.21 = f32[16,128,32,128]{3,2,1,0:T(8,128)} copy(f32[16,128,32,128]{3,1,2,0:T(8,128)} %broadcast_multiply_fusion) | data formatting | bytes 67108864 | tf_op jit(solution)/shard_map/mul | solution.py:37
  959.8 43.4 %fusion.1 = f32[2048,4096]{1,0:T(8,128)} fusion(f32[2048,4096]{1,0:T(8,128)} %fusion.5, f32[256,8,32,128]{3,2,1,0:T(8,128)} %bitcast.73, pred[4096]{0:T(1024)(128)(4,1)S(1)} %fusion.16, pred[2048]{0:T(1024)(128)(4,1)S(1)} %fusion.18), kind=kLoop, calls=%fused_computation.3 | loop fusion | flops 33554432 | bytes 100669440 | tf_op jit(solution)/shard_map/add | solution.py:40
  (28 shorter events, 5.7 us)
Async XLA Ops:
  20.3 46.9 %all-to-all-start.1 = ((bf16[8,7,128,128]{3,2,1,0:T(8,128)(2,1)}), bf16[8,7,128,128]{3,2,1,0:T(8,128)(2,1)S(1)}, u32[]{:S(2)}, u32[]{:S(2)}) async-start(bf16[8,7,128,128]{3,2,1,0:T(8,128)(2,1)} %bitcast.84), calls=%async_computation.1 | async-start | bytes 3670016 | tf_op jit(solution)/shard_map/all_to_all | solution.py:55
  23.9 170.5 %all-gather.10.cloned.1.call-start = ((), (), s32[]{:S(2)}) async-start(), calls=%async_computation.3 | async-start | bytes 6291456 | tf_op jit(solution)/shard_map/all_gather | solution.py:15
  114.8 47.5 %copy-start.1 = (f32[2,512,512]{2,1,0:T(8,128)S(1)}, f32[2,512,512]{2,1,0:T(8,128)}, u32[]{:S(2)}) copy-start(f32[2,512,512]{2,1,0:T(8,128)} %param.21) | copy-start | bytes 6291460
  151.3 11.1 %copy-start = (f32[256,8,32,128]{3,1,2,0:T(8,128)}, f32[256,8,32,128]{3,1,2,0:T(8,128)S(1)}, u32[]{:S(2)}) copy-start(f32[256,8,32,128]{3,1,2,0:T(8,128)S(1)} %copy.33) | copy-start | bytes 100663296
  171.0 302.3 %all-gather.8.cloned.1.call-start = ((), (), s32[]{:S(2)}) async-start(), calls=%async_computation.2 | async-start | bytes 20971520 | tf_op jit(solution)/shard_map/all_gather | solution.py:15
  187.0 419.6 %all-gather.12.cloned.1.call-start = ((), (), s32[]{:S(2)}) async-start(), calls=%async_computation.4 | async-start | bytes 6291456 | tf_op jit(solution)/shard_map/all_gather | solution.py:15
  593.2 301.4 %all-gather.14.cloned.1.call-start = ((), (), s32[]{:S(2)}) async-start(), calls=%async_computation.5 | async-start | bytes 20971520 | tf_op jit(solution)/shard_map/all_gather | solution.py:15
Sparse Core Ops, SparseCore 0:
  171.1 12.5 all-gather.9
  187.1 286.1 all-gather.7
  593.4 11.8 all-gather.11
  606.7 287.9 all-gather.13
